TPU v7x, 32 devices: a whole 2x2x4 slice. The times are simulated.
32 devices in a mesh: mod: 4 (over z), frm: 2 (over x), ori: 4 (over y, core).
Axes of the slice: x: 2, y: 2, z: 4, core: 2. Of those that a mesh axis runs over, the one named last changes fastest.
Arguments:
- counts: int32 [512, 128, 128], P(('frm', 'ori'), 'mod'), may hold values from 0 to 8
- slice_codes: int32 [4096, 128, 128], P('ori', ('mod', 'frm')), may hold values from 0 to 2047
- pixel_mask: int32 [128, 128], P('mod'), may hold values 0 or 1
Outputs:
- log_posterior: float32 [2, 256, 4096], P('frm', 'mod', 'ori')
All inputs are finite; a program needn't handle non-finite values. No bound on the sum of `pixel_mask` on one device may be relied on, other than what follows from the above.
Results may differ from a plain program's by a relative error of at most 0.0024.
Values may be sent and summed in bfloat16 or wider, within the bound.
A program may use at most 64 MiB of HBM per device.

v0:
```python
import functools
import math

import jax
import jax.numpy as jnp
from jax import lax
from jax.experimental import pallas as pl
from jax.experimental.pallas import tpu as pltpu
from jax.sharding import PartitionSpec as P

PASSES = 8
TIME_STEP = 0.2
EDGE_SCALE = 2.0
LOG_FLOOR = -7.0
CODE_STEP = 1.0 / 256.0
GROUPS = 2
STRIDE_ROWS = 8
SLICE_CHUNK = 128
MESH = pl.DeviceIdType.MESH


SQUARE = EDGE_SCALE * EDGE_SCALE


def conduct(d):
    return d / (SQUARE + d * d)


def conduct_pair(a, b):
    return (a + b) * (SQUARE + a * b) / ((SQUARE + a * a) * (SQUARE + b * b))


def flip(h, b):
    return h + b - 2 * b * lax.rem(h // b, 2)


def kernel(
    dims, counts, codes, mask, out,
    codes_v, logs, inten, halo_s, halo_r, band_s, frames, cross, xrecv, zrecv,
    stat_s, stat_r, totals,
    code_sem, hs_sem, hr_sem, own_sem, gs_sem, gr_sem, xs_sem, xr_sem, zs_sem, zr_sem,
    ts_sem, tr_sem,
):
    nm, nf, no, fr, rows, orient, band = dims
    m, f, o = lax.axis_index("mod"), lax.axis_index("frm"), lax.axis_index("ori")
    sizes = {"mod": (m, nm), "frm": (f, nf), "ori": (o, no)}
    lanes = counts.shape[1]
    depth = band * lanes
    high = rows + 2 * PASSES
    gsz = fr // GROUPS
    group = no * fr
    share = group // nm
    chunks = orient // SLICE_CHUNK

    def other(axis, d):
        me, n = sizes[axis]
        return lax.rem(me + d, n)

    def code_copy(c):
        span = SLICE_CHUNK * band
        at = pl.ds(c * span, span)
        return pltpu.make_async_copy(codes.at[at], codes_v.at[at], code_sem.at[c])

    for c in range(chunks):
        code_copy(c).start()

    barrier = pltpu.get_barrier_semaphore()
    for axis in ("mod", "frm", "ori"):
        for d in range(1, sizes[axis][1]):
            pl.semaphore_signal(
                barrier, inc=1, device_id={axis: other(axis, d)}, device_id_type=MESH
            )

    def load_row(i, carry):
        inten[PASSES + i] = counts[pl.ds(i, fr, stride=rows), :].astype(jnp.float32)
        return carry

    lax.fori_loop(0, rows, load_row, 0)
    inten[pl.ds(high, STRIDE_ROWS)] = jnp.zeros((STRIDE_ROWS, fr, lanes), jnp.float32)
    for i in range(PASSES):
        halo_s[0, i] = inten[PASSES + i].astype(jnp.bfloat16)
        halo_s[1, i] = inten[rows + i].astype(jnp.bfloat16)
    pl.semaphore_wait(barrier, nm + nf + no - 3)

    def halo_copy(side):
        return pltpu.make_async_remote_copy(
            src_ref=halo_s.at[side],
            dst_ref=halo_r.at[1 - side],
            send_sem=hs_sem.at[side],
            recv_sem=hr_sem.at[1 - side],
            device_id={"mod": other("mod", nm - 1 if side == 0 else 1)},
            device_id_type=MESH,
        )

    first, last = m == 0, m == nm - 1

    @pl.when(jnp.logical_not(first))
    def _():
        halo_copy(0).start()

    @pl.when(jnp.logical_not(last))
    def _():
        halo_copy(1).start()

    def slice_chunk(c):
        code_copy(c).wait()
        base = c * (SLICE_CHUNK * band)
        acc = jnp.zeros((SLICE_CHUNK, lanes), jnp.float32)
        for s in range(band):
            raw = codes_v[pl.ds(base + s, SLICE_CHUNK, stride=band), :]
            value = (LOG_FLOOR + raw.astype(jnp.float32) * CODE_STEP).astype(jnp.bfloat16)
            logs[pl.ds(c * SLICE_CHUNK, SLICE_CHUNK), pl.ds(s * lanes, lanes)] = value
            weight = mask[pl.ds(f * band + s, 1), :].astype(jnp.float32)
            acc = acc + jnp.exp(value.astype(jnp.float32)) * weight
        totals[:, pl.ds(c * SLICE_CHUNK, SLICE_CHUNK)] = jnp.sum(acc.T, axis=0, keepdims=True)

    early = chunks // 2
    for c in range(early):
        slice_chunk(c)

    @pl.when(first)
    def _():
        inten[pl.ds(0, PASSES)] = jnp.zeros((PASSES, fr, lanes), jnp.float32)

    @pl.when(jnp.logical_not(first))
    def _():
        halo_copy(1).wait_recv()
        inten[pl.ds(0, PASSES)] = halo_r[0].astype(jnp.float32)
        halo_copy(0).wait_send()

    @pl.when(last)
    def _():
        inten[pl.ds(PASSES + rows, PASSES)] = jnp.zeros((PASSES, fr, lanes), jnp.float32)

    @pl.when(jnp.logical_not(last))
    def _():
        halo_copy(0).wait_recv()
        inten[pl.ds(PASSES + rows, PASSES)] = halo_r[1].astype(jnp.float32)
        halo_copy(1).wait_send()

    lane = lax.broadcasted_iota(jnp.int32, (gsz, lanes), 1)
    at_left, at_right = lane == 0, lane == lanes - 1
    row_min = jnp.where(first, PASSES, 0)
    row_max = jnp.where(last, PASSES + rows, high)

    def diffuse(g):
        part = pl.ds(g * gsz, gsz)

        def one_pass(p, carry):
            centre = inten[p + 1, part, :]
            before = conduct(centre - inten[p, part, :])

            def some_rows(k, state):
                c, before = state
                i = p + 1 + STRIDE_ROWS * k
                below = [inten[i + r + 1, part, :] for r in range(STRIDE_ROWS)]
                fresh = []
                for r in range(STRIDE_ROWS):
                    after = conduct(below[r] - c)
                    left = jnp.where(at_left, 0.0, pltpu.roll(c, 1, 1))
                    right = jnp.where(at_right, 0.0, pltpu.roll(c, lanes - 1, 1))
                    side = conduct_pair(left - c, right - c)
                    inside = jnp.logical_and(i + r >= row_min, i + r < row_max)
                    step = jnp.where(inside, TIME_STEP * SQUARE, 0.0)
                    fresh.append(c + step * ((after - before) + side))
                    c, before = below[r], after
                for r in range(STRIDE_ROWS):
                    inten[i + r, part, :] = fresh[r]
                return c, before

            trips = (high - 2 * p - 3 + STRIDE_ROWS) // STRIDE_ROWS
            lax.fori_loop(0, trips, some_rows, (centre, before))
            return carry

        lax.fori_loop(0, PASSES, one_pass, 0)
        for i in range(rows):
            good = mask[i : i + 1, :].astype(jnp.float32)
            band_s[
                pl.ds((i // band) * fr + g * gsz, gsz), pl.ds((i % band) * lanes, lanes)
            ] = (inten[PASSES + i, part, :] * good).astype(jnp.bfloat16)

    def slot(ff, oo, g):
        return frames.at[pl.ds((ff * no + oo) * fr + g * gsz, gsz)]

    pending = []
    count = [0]

    def arrived(ff, oo, g):
        pltpu.make_async_remote_copy(
            src_ref=slot(ff, oo, g), dst_ref=slot(ff, oo, g),
            send_sem=gs_sem.at[0], recv_sem=gr_sem.at[ff * no + oo, g],
            device_id={"ori": other("ori", 1)}, device_id_type=MESH,
        ).wait_recv()

    def send(src, ff, oo, g, target):
        copy = pltpu.make_async_remote_copy(
            src_ref=src, dst_ref=slot(ff, oo, g),
            send_sem=gs_sem.at[count[0]], recv_sem=gr_sem.at[ff * no + oo, g],
            device_id=target, device_id_type=MESH,
        )
        count[0] += 1
        copy.start()
        pending.append(copy)

    def banded(ff, g):
        return band_s.at[pl.ds(ff * fr + g * gsz, gsz)]

    bits = []
    b = no // 2
    while b >= 1:
        bits.append(b)
        b //= 2

    held = [[o]]
    for b in bits:
        held.append(held[-1] + [flip(h, b) for h in held[-1]])

    def first_hop(g):
        for d in range(1, nf):
            fd = other("frm", d)
            send(banded(fd, g), f, o, g, {"frm": fd})
        own = pltpu.make_async_copy(banded(f, g), slot(f, o, g), own_sem.at[g])
        own.start()
        send(banded(f, g), f, o, g, {"ori": flip(o, bits[0])})
        own.wait()

    def second_hop(g):
        for d in range(1, nf):
            fd = other("frm", d)
            arrived(fd, o, g)
            send(slot(fd, o, g), fd, o, g, {"ori": flip(o, bits[0])})

    def take(k, g):
        for d in range(nf):
            for h in held[k][len(held[k]) // 2 :]:
                arrived(other("frm", d), h, g)

    def later_hop(k, g):
        take(k, g)
        if k < len(bits):
            for d in range(nf):
                for h in held[k]:
                    send(slot(other("frm", d), h, g), other("frm", d), h, g, {"ori": flip(o, bits[k])})

    hops = len(bits)
    for step in range(GROUPS):
        diffuse(step)
        first_hop(step)
        if step >= 1:
            second_hop(step - 1)
        if step >= 2:
            later_hop(1, step - 2)
    for c in range(early, early + (chunks - early + 1) // 2):
        slice_chunk(c)
    second_hop(GROUPS - 1)
    later_hop(1, GROUPS - 2)
    for c in range(early + (chunks - early + 1) // 2, chunks):
        slice_chunk(c)
    later_hop(1, GROUPS - 1)
    for k in range(2, hops + 1):
        for g in range(GROUPS):
            later_hop(k, g)

    tile = 256
    order = list(range(nm - 1, -1, -1))

    def target(q):
        mm, b = m, 1
        while b < nm:
            mm = flip(mm, b) if q & b else mm
            b *= 2
        return mm

    def multiply(ff):
        start = pl.multiple_of(ff * group, group)

        def one_tile(t, carry):
            at = pl.multiple_of(t * tile, tile)
            cross[pl.ds(start, group), pl.ds(at, tile)] = (
                lax.dot_general(
                    frames[pl.ds(start, group), :],
                    logs[pl.ds(at, tile), :],
                    (((1,), (1,)), ((), ())),
                    preferred_element_type=jnp.float32,
                )
                - totals[:, pl.ds(at, tile)]
            )
            return carry

        lax.fori_loop(0, orient // tile, one_tile, 0)

    def part_of(ref, ff, mm):
        return ref.at[pl.ds(ff * group + mm * share, share)]

    def x_copy(src_f, dst_f, mm, n):
        return pltpu.make_async_remote_copy(
            src_ref=part_of(cross, dst_f, mm), dst_ref=part_of(xrecv, src_f, mm),
            send_sem=xs_sem.at[n], recv_sem=xr_sem.at[src_f, mm],
            device_id={"frm": dst_f}, device_id_type=MESH,
        )

    n = 0
    for d in range(1, nf):
        fd = other("frm", d)
        multiply(fd)
        for q in order:
            copy = x_copy(f, fd, target(q), n)
            copy.start()
            pending.append(copy)
            n += 1
    multiply(f)

    def z_copy(q):
        return pltpu.make_async_remote_copy(
            src_ref=part_of(cross, f, target(q)), dst_ref=zrecv.at[q],
            send_sem=zs_sem.at[q], recv_sem=zr_sem.at[q],
            device_id={"mod": flip(m, q & -q)}, device_id_type=MESH,
        )

    score = None
    for q in order:
        mm = target(q)
        at = pl.ds(pl.multiple_of(f * group + mm * share, share), share)
        value = cross[at, :]
        for d in range(1, nf):
            fd = other("frm", d)
            x_copy(fd, other("frm", 1), mm, 0).wait_recv()
            value = value + xrecv[pl.ds(pl.multiple_of(fd * group + mm * share, share), share), :]
        b = 1
        while b < nm and not q & b:
            z_copy(q | b).wait_recv()
            value = value + zrecv[q | b]
            b *= 2
        if q == 0:
            score = value
        else:
            cross[at, :] = value
            copy = z_copy(q)
            copy.start()
            pending.append(copy)
    score = score * (1.0 / math.sqrt(rows * nm * lanes))
    peak = jnp.max(score, axis=1, keepdims=True)
    mass = jnp.sum(jnp.exp(score - peak), axis=1, keepdims=True)
    wide = lax.broadcasted_iota(jnp.int32, (share, 128), 1)
    stat_s[...] = jnp.where(wide < 64, peak, mass)

    def t_copy(src_o, dst_o, n):
        return pltpu.make_async_remote_copy(
            src_ref=stat_s, dst_ref=stat_r.at[src_o],
            send_sem=ts_sem.at[n], recv_sem=tr_sem.at[src_o],
            device_id={"ori": dst_o}, device_id_type=MESH,
        )

    for d in range(1, no):
        copy = t_copy(o, other("ori", d), d)
        copy.start()
        pending.append(copy)
    peaks, masses = [peak], [mass]
    for d in range(1, no):
        od = other("ori", d)
        t_copy(od, od, 0).wait_recv()
        got = stat_r[od]
        peaks.append(got[:, 0:1])
        masses.append(got[:, 64:65])
    top = functools.reduce(jnp.maximum, peaks)
    weight = sum(s * jnp.exp(p - top) for p, s in zip(peaks, masses))
    out[...] = score - (top + jnp.log(weight))
    for copy in pending:
        copy.wait_send()


def body(counts, slice_codes, pixel_mask):
    nm, nf, no = (lax.axis_size(a) for a in ("mod", "frm", "ori"))
    fr, rows, lanes = counts.shape
    orient, band, _ = slice_codes.shape
    group = no * fr
    share = group // nm
    depth = band * lanes
    high = rows + 2 * PASSES
    dims = (nm, nf, no, fr, rows, orient, band)
    dma = pltpu.SemaphoreType.DMA
    f32, bf16 = jnp.float32, jnp.bfloat16
    vmem = pl.BlockSpec(memory_space=pltpu.VMEM)
    result = pl.pallas_call(
        functools.partial(kernel, dims),
        out_shape=jax.ShapeDtypeStruct((share, orient), f32),
        in_specs=[vmem, pl.BlockSpec(memory_space=pl.ANY), vmem],
        out_specs=vmem,
        scratch_shapes=[
            pltpu.VMEM((orient * band, lanes), jnp.int32),
            pltpu.VMEM((orient, depth), bf16),
            pltpu.VMEM((high + STRIDE_ROWS, fr, lanes), f32),
            pltpu.VMEM((2, PASSES, fr, lanes), bf16),
            pltpu.VMEM((2, PASSES, fr, lanes), bf16),
            pltpu.VMEM((nf * fr, depth), bf16),
            pltpu.VMEM((nf * group, depth), bf16),
            pltpu.VMEM((nf * group, orient), f32),
            pltpu.VMEM((nf * group, orient), f32),
            pltpu.VMEM((nm, share, orient), f32),
            pltpu.VMEM((share, 128), f32),
            pltpu.VMEM((no, share, 128), f32),
            pltpu.VMEM((1, orient), f32),
            dma((orient // SLICE_CHUNK,)),
            dma((2,)),
            dma((2,)),
            dma((GROUPS,)),
            dma((GROUPS * nf * (no + 1),)),
            dma((nf * no, GROUPS)),
            dma((nf * nm,)),
            dma((nf, nm)),
            dma((nm,)),
            dma((nm,)),
            dma((no,)),
            dma((no,)),
        ],
        compiler_params=pltpu.CompilerParams(collective_id=0, has_side_effects=True),
    )(counts.reshape(fr * rows, lanes), slice_codes.reshape(orient * band, lanes), pixel_mask)
    return result[None]


def solution(mesh):
    in_specs = (P(("frm", "ori"), "mod", None), P("ori", ("mod", "frm"), None), P("mod", None))
    out_specs = P("frm", "mod", "ori")
    return jax.shard_map(body, mesh=mesh, in_specs=in_specs, out_specs=out_specs, check_vma=False)
```

profile of v0, /device:TPU:0, one launch (start us, length us, event | category | flops | bytes accessed | tf_op | source)
XLA Modules:
  0.0 73.2 jit_solution(5178958305197278460)
XLA Ops:
  0.0 71.6 %shard_map.37 = f32[64,1024]{1,0:T(8,128)} custom-call(s32[2048,128]{1,0:T(8,128)} %bitcast.4, s32[16384,128]{1,0:T(8,128)} %bitcast.3, s32[32,128]{1,0:T(8,128)} %mask.1), custom_call_target="tpu_custom_call" | custom-call | tf_op jit(solution)/shard_map/pallas_call | solution.py:384
  71.6 1.7 %copy.5 = f32[1,64,1024]{2,1,0:T(8,128)} copy(f32[1,64,1024]{2,1,0:T(8,128)} %bitcast.5) | data formatting | bytes 524288
where the time goes:
time: 73.4 us; the launch traced here: 73.2 us
  Pallas kernels  71.6 us (98%)
  local copies, waits for them, and re-layouts  1.67 us (2%)
    pallas_call x1, Pallas kernels, body(): pl.pallas_call(functools.partial(kernel, dims), out_shape=jax.ShapeDtypeS...  71.6 us
    unnamed x1, local copies, waits for them, and re-layouts  1.67 us

commit v1 on v0

v1 whole, which is shorter than its diff:
```python
import functools
import math

import jax
import jax.numpy as jnp
from jax import lax
from jax.experimental import pallas as pl
from jax.experimental.pallas import tpu as pltpu
from jax.sharding import PartitionSpec as P

PASSES = 8
TIME_STEP = 0.2
EDGE_SCALE = 2.0
LOG_FLOOR = -7.0
CODE_STEP = 1.0 / 256.0
GROUPS = 2
STRIDE_ROWS = 8
SLICE_CHUNK = 128
MESH = pl.DeviceIdType.MESH


SQUARE = EDGE_SCALE * EDGE_SCALE
DENOM = 1.0 / TIME_STEP
SCALE = math.sqrt(DENOM / SQUARE)
TILE = 256


def flux(v):
    return v / (DENOM + v * v)


def flip(h, b):
    return h + b - 2 * b * lax.rem(h // b, 2)


def group_count(nm, no, fr):
    count = 4
    while count > 1 and (nm > no or no % nm or fr % (16 * count)):
        count //= 2
    return count


def kernel(
    dims, counts, codes, mask, out,
    codes_v, logs, inten, halo_s, halo_r, band_s, frames, cross, centre, xs, xr, zs, zr,
    score, stat_s, stat_r, totals,
    code_sem, hs_sem, hr_sem, own_sem, gs_sem, gr_sem, xs_sem, xr_sem, zs_sem, zr_sem,
    ts_sem, tr_sem,
):
    nm, nf, no, fr, rows, orient, band, groups = dims
    m, f, o = lax.axis_index("mod"), lax.axis_index("frm"), lax.axis_index("ori")
    sizes = {"mod": (m, nm), "frm": (f, nf), "ori": (o, no)}
    lanes = counts.shape[1]
    high = rows + 2 * PASSES
    gsz = fr // groups
    gg = no * gsz
    sg = gg // nm
    chunks = orient // SLICE_CHUNK
    tiles = orient // TILE
    f32, bf16 = jnp.float32, jnp.bfloat16

    def other(axis, d):
        me, n = sizes[axis]
        return lax.rem(me + d, n)

    def code_copy(c):
        span = SLICE_CHUNK * band
        at = pl.ds(c * span, span)
        return pltpu.make_async_copy(codes.at[at], codes_v.at[at], code_sem.at[c])

    for c in range(chunks):
        code_copy(c).start()

    barrier = pltpu.get_barrier_semaphore()
    for axis in ("mod", "frm", "ori"):
        for d in range(1, sizes[axis][1]):
            pl.semaphore_signal(
                barrier, inc=1, device_id={axis: other(axis, d)}, device_id_type=MESH
            )

    def count_row(i):
        return counts[pl.ds(i, fr, stride=rows), :].astype(f32)

    for i in range(PASSES):
        halo_s[0, i] = count_row(i).astype(bf16)
        halo_s[1, i] = count_row(rows - PASSES + i).astype(bf16)
    pl.semaphore_wait(barrier, nm + nf + no - 3)

    first, last = m == 0, m == nm - 1

    def part(g):
        return pl.ds(g * gsz, gsz)

    def halo_copy(side, g):
        return pltpu.make_async_remote_copy(
            src_ref=halo_s.at[side, :, part(g), :],
            dst_ref=halo_r.at[1 - side, :, part(g), :],
            send_sem=hs_sem.at[side, g],
            recv_sem=hr_sem.at[1 - side, g],
            device_id={"mod": other("mod", nm - 1 if side == 0 else 1)},
            device_id_type=MESH,
        )

    @pl.when(jnp.logical_not(first))
    def _():
        for g in range(groups):
            halo_copy(0, g).start()

    @pl.when(jnp.logical_not(last))
    def _():
        for g in range(groups):
            halo_copy(1, g).start()

    def load_row(i, carry):
        inten[PASSES + i] = count_row(i) * SCALE
        return carry

    lax.fori_loop(0, rows, load_row, 0)
    inten[pl.ds(high, STRIDE_ROWS)] = jnp.zeros((STRIDE_ROWS, fr, lanes), f32)

    def slice_chunk(c):
        code_copy(c).wait()
        base = c * (SLICE_CHUNK * band)
        acc = jnp.zeros((SLICE_CHUNK, lanes), f32)
        for s in range(band):
            raw = codes_v[pl.ds(base + s, SLICE_CHUNK, stride=band), :]
            value = (LOG_FLOOR + raw.astype(f32) * CODE_STEP).astype(bf16)
            logs[pl.ds(c * SLICE_CHUNK, SLICE_CHUNK), pl.ds(s * lanes, lanes)] = value
            weight = mask[pl.ds(f * band + s, 1), :].astype(f32)
            acc = acc + jnp.exp(value.astype(f32)) * weight
        totals[:, pl.ds(c * SLICE_CHUNK, SLICE_CHUNK)] = jnp.sum(acc.T, axis=0, keepdims=True)

    def halo_in(g):
        @pl.when(first)
        def _():
            inten[pl.ds(0, PASSES), part(g), :] = jnp.zeros((PASSES, gsz, lanes), f32)

        @pl.when(jnp.logical_not(first))
        def _():
            halo_copy(1, g).wait_recv()
            inten[pl.ds(0, PASSES), part(g), :] = halo_r[0, :, part(g), :].astype(f32) * SCALE
            halo_copy(0, g).wait_send()

        @pl.when(last)
        def _():
            inten[pl.ds(PASSES + rows, PASSES), part(g), :] = jnp.zeros((PASSES, gsz, lanes), f32)

        @pl.when(jnp.logical_not(last))
        def _():
            halo_copy(0, g).wait_recv()
            inten[pl.ds(PASSES + rows, PASSES), part(g), :] = (
                halo_r[1, :, part(g), :].astype(f32) * SCALE
            )
            halo_copy(1, g).wait_send()

    lane = lax.broadcasted_iota(jnp.int32, (gsz, lanes), 1)
    at_left, at_right = lane == 0, lane == lanes - 1

    def diffuse(g):
        halo_in(g)
        at = part(g)

        def one_pass(p, carry):
            low = jnp.where(first, PASSES, p + 1)
            top = jnp.where(last, PASSES + rows, high - 1 - p)
            c = inten[low, at, :]
            before = flux(c - inten[low - 1, at, :])

            def some_rows(k, state):
                c, before = state
                i = low + STRIDE_ROWS * k
                below = [inten[i + r + 1, at, :] for r in range(STRIDE_ROWS)]
                fresh = []
                for r in range(STRIDE_ROWS):
                    after = flux(below[r] - c)
                    right = jnp.where(at_right, 0.0, pltpu.roll(c, lanes - 1, 1))
                    east = flux(right - c)
                    west = jnp.where(at_left, flux(c), pltpu.roll(east, 1, 1))
                    fresh.append(c + ((after - before) + (east - west)))
                    c, before = below[r], after
                for r in range(STRIDE_ROWS):
                    inten[i + r, at, :] = fresh[r]
                return c, before

            trips = (top - low + STRIDE_ROWS - 1) // STRIDE_ROWS
            lax.fori_loop(0, trips, some_rows, (c, before))
            edge = inten[PASSES + rows, at, :]
            inten[PASSES + rows, at, :] = jnp.where(last, 0.0, edge)
            return carry

        lax.fori_loop(0, PASSES, one_pass, 0)
        for i in range(rows):
            good = mask[i : i + 1, :].astype(f32) * (1.0 / SCALE)
            band_s[
                pl.ds((i // band) * fr + g * gsz, gsz), pl.ds((i % band) * lanes, lanes)
            ] = (inten[PASSES + i, at, :] * good).astype(bf16)

    def slot(ff, oo, g):
        return frames.at[pl.ds(((g * nf + ff) * no + oo) * gsz, gsz)]

    pending = []
    count = [0]

    def arrived(ff, oo, g):
        pltpu.make_async_remote_copy(
            src_ref=slot(ff, oo, g), dst_ref=slot(ff, oo, g),
            send_sem=gs_sem.at[0], recv_sem=gr_sem.at[ff * no + oo, g],
            device_id={"ori": other("ori", 1)}, device_id_type=MESH,
        ).wait_recv()

    def send(src, ff, oo, g, target):
        copy = pltpu.make_async_remote_copy(
            src_ref=src, dst_ref=slot(ff, oo, g),
            send_sem=gs_sem.at[count[0]], recv_sem=gr_sem.at[ff * no + oo, g],
            device_id=target, device_id_type=MESH,
        )
        count[0] += 1
        copy.start()
        pending.append(copy)

    def banded(ff, g):
        return band_s.at[pl.ds(ff * fr + g * gsz, gsz)]

    bits = []
    b = no // 2
    while b >= 1:
        bits.append(b)
        b //= 2
    hops = len(bits)

    held = [[o]]
    for b in bits:
        held.append(held[-1] + [flip(h, b) for h in held[-1]])

    def first_hop(g):
        for d in range(1, nf):
            fd = other("frm", d)
            send(banded(fd, g), f, o, g, {"frm": fd})
        send(banded(f, g), f, o, g, {"ori": flip(o, bits[0])})
        own = pltpu.make_async_copy(banded(f, g), slot(f, o, g), own_sem.at[g])
        own.start()
        own.wait()

    def second_hop(g):
        for d in range(1, nf):
            fd = other("frm", d)
            arrived(fd, o, g)
            send(slot(fd, o, g), fd, o, g, {"ori": flip(o, bits[0])})

    def later_hop(k, g):
        for d in range(nf):
            for h in held[k][len(held[k]) // 2 :]:
                arrived(other("frm", d), h, g)
        if k < hops:
            for d in range(nf):
                for h in held[k]:
                    send(slot(other("frm", d), h, g), other("frm", d), h, g, {"ori": flip(o, bits[k])})

    def mine(ff):
        return pl.ds(pl.multiple_of(ff * gg, gg), gg)

    def columns(t):
        return pl.ds(t * TILE, TILE)

    def sent_columns(t):
        return pl.ds(0, lanes + TILE) if t == 0 else pl.ds(lanes + t * TILE, TILE)

    def x_copy(src_f, dst_f, g, t, n):
        return pltpu.make_async_remote_copy(
            src_ref=xs.at[g, dst_f, :, sent_columns(t)],
            dst_ref=xr.at[g, src_f, :, sent_columns(t)],
            send_sem=xs_sem.at[g, n, t], recv_sem=xr_sem.at[g, src_f, t],
            device_id={"frm": dst_f}, device_id_type=MESH,
        )

    def multiply(g, t):
        value = lax.dot_general(
            frames[pl.ds(g * nf * gg, nf * gg), :],
            logs[columns(t), :],
            (((1,), (1,)), ((), ())),
            preferred_element_type=f32,
        ) - totals[:, columns(t)]
        cross[g, :, columns(t)] = value
        if t == 0:
            mean = jnp.mean(value, axis=1, keepdims=True).astype(bf16).astype(f32)
            centre[g] = jnp.broadcast_to(mean, (nf * gg, lanes))
        for d in range(1, nf):
            fd = other("frm", d)
            middle = centre[g, mine(fd), :]
            if t == 0:
                xs[g, fd, :, pl.ds(0, lanes)] = middle.astype(bf16)
            for j in range(TILE // lanes):
                at = t * TILE + j * lanes
                xs[g, fd, :, pl.ds(lanes + at, lanes)] = (
                    cross[g, mine(fd), pl.ds(at, lanes)] - middle
                ).astype(bf16)
            copy = x_copy(f, fd, g, t, d)
            copy.start()
            pending.append(copy)

    def z_copy(src_m, dst_m, g, t, n):
        return pltpu.make_async_remote_copy(
            src_ref=zs.at[g, pl.ds(pl.multiple_of(dst_m * sg, sg), sg), sent_columns(t)],
            dst_ref=zr.at[g, src_m, :, sent_columns(t)],
            send_sem=zs_sem.at[g, n, t], recv_sem=zr_sem.at[g, src_m, t],
            device_id={"mod": dst_m}, device_id_type=MESH,
        )

    def reduce_frm(g, t):
        for d in range(1, nf):
            fd = other("frm", d)
            x_copy(fd, f, g, t, 0).wait_recv()
        parts = [(xr, other("frm", d)) for d in range(1, nf)]
        mids = [r[g, i, :, pl.ds(0, lanes)].astype(f32) for r, i in parts]
        middle = sum(mids, centre[g, mine(f), :]).astype(bf16).astype(f32)
        if t == 0:
            zs[g, :, pl.ds(0, lanes)] = middle.astype(bf16)
        for j in range(TILE // lanes):
            at = t * TILE + j * lanes
            value = cross[g, mine(f), pl.ds(at, lanes)]
            for (r, i), mid in zip(parts, mids):
                value = value + (r[g, i, :, pl.ds(lanes + at, lanes)].astype(f32) + mid)
            cross[g, mine(f), pl.ds(at, lanes)] = value
            zs[g, :, pl.ds(lanes + at, lanes)] = (value - middle).astype(bf16)
        for d in range(1, nm):
            copy = z_copy(m, other("mod", d), g, t, d)
            copy.start()
            pending.append(copy)

    wide = lax.broadcasted_iota(jnp.int32, (sg, 128), 1)

    def t_copy(src_o, dst_o, g, n):
        return pltpu.make_async_remote_copy(
            src_ref=stat_s.at[g], dst_ref=stat_r.at[g, src_o],
            send_sem=ts_sem.at[g, n], recv_sem=tr_sem.at[g, src_o],
            device_id={"ori": dst_o}, device_id_type=MESH,
        )

    def reduce_mod(g):
        for t in range(tiles):
            for d in range(1, nm):
                z_copy(other("mod", d), m, g, t, 0).wait_recv()
        at = pl.ds(pl.multiple_of(f * gg + m * sg, sg), sg)
        value = cross[g, at, :]
        for d in range(1, nm):
            md = other("mod", d)
            value = value + (
                zr[g, md, :, pl.ds(lanes, orient)].astype(f32) + zr[g, md, :, pl.ds(0, 1)].astype(f32)
            )
        value = value * (1.0 / math.sqrt(rows * nm * lanes))
        score[g] = value
        peak = jnp.max(value, axis=1, keepdims=True)
        mass = jnp.sum(jnp.exp(value - peak), axis=1, keepdims=True)
        stat_s[g] = jnp.where(wide < 64, peak, mass)
        for d in range(1, no):
            copy = t_copy(o, other("ori", d), g, d)
            copy.start()
            pending.append(copy)

    def finish(g):
        got = [stat_s[g]]
        for d in range(1, no):
            od = other("ori", d)
            t_copy(od, o, g, 0).wait_recv()
            got.append(stat_r[g, od])
        peaks, masses = [s[:, 0:1] for s in got], [s[:, 64:65] for s in got]
        top = functools.reduce(jnp.maximum, peaks)
        weight = sum(s * jnp.exp(p - top) for p, s in zip(peaks, masses))
        value = score[g] - (top + jnp.log(weight))
        blocks = 1 if groups == 1 else no // nm
        span = sg // blocks
        for s in range(blocks):
            out[pl.ds(s * fr + g * gsz, span), :] = value[s * span : (s + 1) * span, :]

    early = chunks // 2
    tasks = []

    def task(when, call, *args):
        tasks.append((when, len(tasks), call, args))

    for c in range(chunks):
        task(-1.0 if c < early else 0.6, slice_chunk, c)
    for g in range(groups):
        task(g, diffuse, g)
        task(g + 0.1, first_hop, g)
        task(g + 1.2, second_hop, g)
        for k in range(1, hops + 1):
            task(g + 1.3 + 0.95 * k, later_hop, k, g)
        for t in range(tiles):
            task(g + 1.4 + 0.95 * hops, multiply, g, t)
        for t in range(tiles):
            task(g + 2.5 + 0.95 * hops, reduce_frm, g, t)
        task(g + 3.6 + 0.95 * hops, reduce_mod, g)
        task(g + 4.7 + 0.95 * hops, finish, g)
    for _, _, call, args in sorted(tasks, key=lambda entry: entry[:2]):
        call(*args)
    for copy in pending:
        copy.wait_send()


def body(counts, slice_codes, pixel_mask):
    nm, nf, no = (lax.axis_size(a) for a in ("mod", "frm", "ori"))
    fr, rows, lanes = counts.shape
    orient, band, _ = slice_codes.shape
    group = no * fr
    share = group // nm
    depth = band * lanes
    high = rows + 2 * PASSES
    groups = group_count(nm, no, fr)
    gg = group // groups
    sg = gg // nm
    tiles = orient // TILE
    dims = (nm, nf, no, fr, rows, orient, band, groups)
    dma = pltpu.SemaphoreType.DMA
    f32, bf16 = jnp.float32, jnp.bfloat16
    vmem = pl.BlockSpec(memory_space=pltpu.VMEM)
    result = pl.pallas_call(
        functools.partial(kernel, dims),
        out_shape=jax.ShapeDtypeStruct((share, orient), f32),
        in_specs=[vmem, pl.BlockSpec(memory_space=pl.ANY), vmem],
        out_specs=vmem,
        scratch_shapes=[
            pltpu.VMEM((orient * band, lanes), jnp.int32),
            pltpu.VMEM((orient, depth), bf16),
            pltpu.VMEM((high + STRIDE_ROWS, fr, lanes), f32),
            pltpu.VMEM((2, PASSES, fr, lanes), bf16),
            pltpu.VMEM((2, PASSES, fr, lanes), bf16),
            pltpu.VMEM((nf * fr, depth), bf16),
            pltpu.VMEM((nf * group, depth), bf16),
            pltpu.VMEM((groups, nf * gg, orient), f32),
            pltpu.VMEM((groups, nf * gg, lanes), f32),
            pltpu.VMEM((groups, nf, gg, lanes + orient), bf16),
            pltpu.VMEM((groups, nf, gg, lanes + orient), bf16),
            pltpu.VMEM((groups, gg, lanes + orient), bf16),
            pltpu.VMEM((groups, nm, sg, lanes + orient), bf16),
            pltpu.VMEM((groups, sg, orient), f32),
            pltpu.VMEM((groups, sg, 128), f32),
            pltpu.VMEM((groups, no, sg, 128), f32),
            pltpu.VMEM((1, orient), f32),
            dma((orient // SLICE_CHUNK,)),
            dma((2, groups)),
            dma((2, groups)),
            dma((groups,)),
            dma((groups * nf * (no + 1),)),
            dma((nf * no, groups)),
            dma((groups, nf, tiles)),
            dma((groups, nf, tiles)),
            dma((groups, nm, tiles)),
            dma((groups, nm, tiles)),
            dma((groups, no)),
            dma((groups, no)),
        ],
        compiler_params=pltpu.CompilerParams(collective_id=0, has_side_effects=True),
    )(counts.reshape(fr * rows, lanes), slice_codes.reshape(orient * band, lanes), pixel_mask)
    return result[None]


def solution(mesh):
    in_specs = (P(("frm", "ori"), "mod", None), P("ori", ("mod", "frm"), None), P("mod", None))
    out_specs = P("frm", "mod", "ori")
    return jax.shard_map(body, mesh=mesh, in_specs=in_specs, out_specs=out_specs, check_vma=False)
```

time: 73.4 us -> 74.4 us (1.014)
  Pallas kernels: 71.6 us -> 72.6 us
    pallas_call x1, Pallas kernels: 71.6 us -> 72.6 us  [body(): pl.pallas_call(functools.partial(kernel, dims), out_shape=jax.ShapeDtypeS...]
where the time goes in v1:
time: 74.4 us; the launch traced here: 74.2 us
  Pallas kernels  72.6 us (98%)
  local copies, waits for them, and re-layouts  1.67 us (2%)
    pallas_call x1, Pallas kernels, body(): pl.pallas_call(functools.partial(kernel, dims), out_shape=jax.ShapeDtypeS...  72.6 us
    unnamed x1, local copies, waits for them, and re-layouts  1.67 us

profile of v1, /device:TPU:0, one launch (start us, length us, event | category | flops | bytes accessed | tf_op | source)
XLA Modules:
  0.0 74.2 jit_solution(16431118232795541984)
XLA Ops:
  0.0 72.6 %shard_map.37 = f32[64,1024]{1,0:T(8,128)} custom-call(s32[2048,128]{1,0:T(8,128)} %bitcast.4, s32[16384,128]{1,0:T(8,128)} %bitcast.3, s32[32,128]{1,0:T(8,128)} %mask.1), custom_call_target="tpu_custom_call" | custom-call | tf_op jit(solution)/shard_map/pallas_call | solution.py:417
  72.6 1.7 %copy.5 = f32[1,64,1024]{2,1,0:T(8,128)} copy(f32[1,64,1024]{2,1,0:T(8,128)} %bitcast.5) | data formatting | bytes 524288

commit v2 on v1

--- a/solution.py
+++ b/solution.py
@@ -41,10 +41,10 @@
 
 
 def kernel(
-    dims, counts, codes, mask, out,
-    codes_v, logs, inten, halo_s, halo_r, band_s, frames, cross, centre, xs, xr, zs, zr,
-    score, stat_s, stat_r, totals,
-    code_sem, hs_sem, hr_sem, own_sem, gs_sem, gr_sem, xs_sem, xr_sem, zs_sem, zr_sem,
+    dims, counts_h, codes, mask_h, out,
+    counts, mask, codes_v, logs, inten, halo_s, halo_r, band_s, frames, cross, centre, xs, xr, zs, zr,
+    score, stat_s, stat_r, totals, split, slope,
+    load_sem, know, code_sem, hs_sem, hr_sem, own_sem, gs_sem, gr_sem, xs_sem, xr_sem, zs_sem, zr_sem,
     ts_sem, tr_sem,
 ):
     nm, nf, no, fr, rows, orient, band, groups = dims
@@ -68,15 +68,46 @@
         at = pl.ds(c * span, span)
         return pltpu.make_async_copy(codes.at[at], codes_v.at[at], code_sem.at[c])
 
+    loads = [
+        pltpu.make_async_copy(counts_h, counts, load_sem.at[0]),
+        pltpu.make_async_copy(mask_h, mask, load_sem.at[1]),
+    ]
+    for copy in loads:
+        copy.start()
     for c in range(chunks):
         code_copy(c).start()
 
+    first, last = m == 0, m == nm - 1
+    bits = []
+    b = no // 2
+    while b >= 1:
+        bits.append(b)
+        b //= 2
+    hops = len(bits)
+    links = nf - 1 + hops + jnp.where(first, 0, 1) + jnp.where(last, 0, 1)
+    rounds = max(nm - 1, hops) - 1
+
+    def greet(sem):
+        def hello(target):
+            pl.semaphore_signal(sem, inc=1, device_id=target, device_id_type=MESH)
+
+        @pl.when(jnp.logical_not(first))
+        def _():
+            hello({"mod": other("mod", nm - 1)})
+
+        @pl.when(jnp.logical_not(last))
+        def _():
+            hello({"mod": other("mod", 1)})
+
+        for d in range(1, nf):
+            hello({"frm": other("frm", d)})
+        for b in bits:
+            hello({"ori": flip(o, b)})
+
     barrier = pltpu.get_barrier_semaphore()
-    for axis in ("mod", "frm", "ori"):
-        for d in range(1, sizes[axis][1]):
-            pl.semaphore_signal(
-                barrier, inc=1, device_id={axis: other(axis, d)}, device_id_type=MESH
-            )
+    greet(barrier)
+    for copy in loads:
+        copy.wait()
 
     def count_row(i):
         return counts[pl.ds(i, fr, stride=rows), :].astype(f32)
@@ -84,9 +115,7 @@
     for i in range(PASSES):
         halo_s[0, i] = count_row(i).astype(bf16)
         halo_s[1, i] = count_row(rows - PASSES + i).astype(bf16)
-    pl.semaphore_wait(barrier, nm + nf + no - 3)
-
-    first, last = m == 0, m == nm - 1
+    pl.semaphore_wait(barrier, links)
 
     def part(g):
         return pl.ds(g * gsz, gsz)
@@ -112,11 +141,23 @@
             halo_copy(1, g).start()
 
     def load_row(i, carry):
-        inten[PASSES + i] = count_row(i) * SCALE
+        row = count_row(i) * SCALE
+        for g in range(groups):
+            inten[g, PASSES + i] = row[g * gsz : (g + 1) * gsz]
         return carry
 
     lax.fori_loop(0, rows, load_row, 0)
-    inten[pl.ds(high, STRIDE_ROWS)] = jnp.zeros((STRIDE_ROWS, fr, lanes), f32)
+    inten[:, pl.ds(high, STRIDE_ROWS)] = jnp.zeros((groups, STRIDE_ROWS, gsz, lanes), f32)
+    slope[pl.ds(high, STRIDE_ROWS)] = jnp.zeros((STRIDE_ROWS, gsz, 2 * lanes), f32)
+    if rounds:
+        greet(know.at[0])
+    row_of = lax.rem(lax.broadcasted_iota(jnp.int32, (2 * lanes, 2 * lanes), 0), lanes)
+    col_of = lax.broadcasted_iota(jnp.int32, (2 * lanes, 2 * lanes), 1)
+    here = lax.rem(col_of, lanes)
+    beside = here + jnp.where(col_of < lanes, 1, -1)
+    shifts = (
+        jnp.where(row_of == beside, 1.0, 0.0) - jnp.where(row_of == here, 1.0, 0.0)
+    ).astype(bf16)
 
     def slice_chunk(c):
         code_copy(c).wait()
@@ -133,59 +174,71 @@
     def halo_in(g):
         @pl.when(first)
         def _():
-            inten[pl.ds(0, PASSES), part(g), :] = jnp.zeros((PASSES, gsz, lanes), f32)
+            inten[g, pl.ds(0, PASSES)] = jnp.zeros((PASSES, gsz, lanes), f32)
 
         @pl.when(jnp.logical_not(first))
         def _():
             halo_copy(1, g).wait_recv()
-            inten[pl.ds(0, PASSES), part(g), :] = halo_r[0, :, part(g), :].astype(f32) * SCALE
+            inten[g, pl.ds(0, PASSES)] = halo_r[0, :, part(g), :].astype(f32) * SCALE
             halo_copy(0, g).wait_send()
 
         @pl.when(last)
         def _():
-            inten[pl.ds(PASSES + rows, PASSES), part(g), :] = jnp.zeros((PASSES, gsz, lanes), f32)
+            inten[g, pl.ds(PASSES + rows, PASSES)] = jnp.zeros((PASSES, gsz, lanes), f32)
 
         @pl.when(jnp.logical_not(last))
         def _():
             halo_copy(0, g).wait_recv()
-            inten[pl.ds(PASSES + rows, PASSES), part(g), :] = (
+            inten[g, pl.ds(PASSES + rows, PASSES)] = (
                 halo_r[1, :, part(g), :].astype(f32) * SCALE
             )
             halo_copy(1, g).wait_send()
 
-    lane = lax.broadcasted_iota(jnp.int32, (gsz, lanes), 1)
-    at_left, at_right = lane == 0, lane == lanes - 1
+    def keep(i, value):
+        top = value.astype(bf16)
+        split[i, :, pl.ds(0, lanes)] = top
+        split[i, :, pl.ds(lanes, lanes)] = (value - top.astype(f32)).astype(bf16)
 
     def diffuse(g):
         halo_in(g)
-        at = part(g)
+
+        def keep_row(i, carry):
+            keep(i, inten[g, i])
+            return carry
+
+        lax.fori_loop(0, high, keep_row, 0)
 
         def one_pass(p, carry):
+            slope[pl.ds(0, high)] = lax.dot_general(
+                split[pl.ds(0, high)].reshape(high * gsz, 2 * lanes), shifts,
+                (((1,), (0,)), ((), ())), preferred_element_type=f32,
+            ).reshape(high, gsz, 2 * lanes)
             low = jnp.where(first, PASSES, p + 1)
             top = jnp.where(last, PASSES + rows, high - 1 - p)
-            c = inten[low, at, :]
-            before = flux(c - inten[low - 1, at, :])
+            c = inten[g, low]
+            before = flux(c - inten[g, low - 1])
 
             def some_rows(k, state):
                 c, before = state
                 i = low + STRIDE_ROWS * k
-                below = [inten[i + r + 1, at, :] for r in range(STRIDE_ROWS)]
+                below = [inten[g, i + r + 1] for r in range(STRIDE_ROWS)]
                 fresh = []
                 for r in range(STRIDE_ROWS):
                     after = flux(below[r] - c)
-                    right = jnp.where(at_right, 0.0, pltpu.roll(c, lanes - 1, 1))
-                    east = flux(right - c)
-                    west = jnp.where(at_left, flux(c), pltpu.roll(east, 1, 1))
-                    fresh.append(c + ((after - before) + (east - west)))
+                    side = flux(slope[i + r, :, pl.ds(0, lanes)]) + flux(
+                        slope[i + r, :, pl.ds(lanes, lanes)]
+                    )
+                    fresh.append(c + ((after - before) + side))
                     c, before = below[r], after
                 for r in range(STRIDE_ROWS):
-                    inten[i + r, at, :] = fresh[r]
+                    inten[g, i + r] = fresh[r]
+                    keep(i + r, fresh[r])
                 return c, before
 
             trips = (top - low + STRIDE_ROWS - 1) // STRIDE_ROWS
             lax.fori_loop(0, trips, some_rows, (c, before))
-            edge = inten[PASSES + rows, at, :]
-            inten[PASSES + rows, at, :] = jnp.where(last, 0.0, edge)
+            edge = inten[g, PASSES + rows]
+            inten[g, PASSES + rows] = jnp.where(last, 0.0, edge)
             return carry
 
         lax.fori_loop(0, PASSES, one_pass, 0)
@@ -193,7 +246,7 @@
             good = mask[i : i + 1, :].astype(f32) * (1.0 / SCALE)
             band_s[
                 pl.ds((i // band) * fr + g * gsz, gsz), pl.ds((i % band) * lanes, lanes)
-            ] = (inten[PASSES + i, at, :] * good).astype(bf16)
+            ] = (inten[g, PASSES + i] * good).astype(bf16)
 
     def slot(ff, oo, g):
         return frames.at[pl.ds(((g * nf + ff) * no + oo) * gsz, gsz)]
@@ -220,13 +273,6 @@
 
     def banded(ff, g):
         return band_s.at[pl.ds(ff * fr + g * gsz, gsz)]
-
-    bits = []
-    b = no // 2
-    while b >= 1:
-        bits.append(b)
-        b //= 2
-    hops = len(bits)
 
     held = [[o]]
     for b in bits:
@@ -372,26 +418,34 @@
         for s in range(blocks):
             out[pl.ds(s * fr + g * gsz, span), :] = value[s * span : (s + 1) * span, :]
 
+    def knowing(r):
+        pl.semaphore_wait(know.at[r], links)
+        if r + 1 < rounds:
+            greet(know.at[r + 1])
+
     early = chunks // 2
     tasks = []
 
     def task(when, call, *args):
         tasks.append((when, len(tasks), call, args))
 
+    for r in range(rounds):
+        task(0.3 + 0.1 * r, knowing, r)
     for c in range(chunks):
-        task(-1.0 if c < early else 0.6, slice_chunk, c)
+        task(-1.0 if c < early else 0.6 + (1.0 if 4 * c >= 3 * chunks else 0.0), slice_chunk, c)
     for g in range(groups):
         task(g, diffuse, g)
         task(g + 0.1, first_hop, g)
         task(g + 1.2, second_hop, g)
-        for k in range(1, hops + 1):
-            task(g + 1.3 + 0.95 * k, later_hop, k, g)
+        for k in range(1, hops):
+            task(g + 2.2 + 0.5 * (k - 1), later_hop, k, g)
+        task(g + 2.3 + 0.5 * (hops - 2), later_hop, hops, g)
         for t in range(tiles):
-            task(g + 1.4 + 0.95 * hops, multiply, g, t)
+            task(g + 2.4 + 0.5 * (hops - 2), multiply, g, t)
         for t in range(tiles):
-            task(g + 2.5 + 0.95 * hops, reduce_frm, g, t)
-        task(g + 3.6 + 0.95 * hops, reduce_mod, g)
-        task(g + 4.7 + 0.95 * hops, finish, g)
+            task(g + 3.3 + 0.5 * (hops - 2), reduce_frm, g, t)
+        task(g + 4.2 + 0.5 * (hops - 2), reduce_mod, g)
+        task(g + 4.9 + 0.5 * (hops - 2), finish, g)
     for _, _, call, args in sorted(tasks, key=lambda entry: entry[:2]):
         call(*args)
     for copy in pending:
@@ -413,16 +467,16 @@
     dims = (nm, nf, no, fr, rows, orient, band, groups)
     dma = pltpu.SemaphoreType.DMA
     f32, bf16 = jnp.float32, jnp.bfloat16
-    vmem = pl.BlockSpec(memory_space=pltpu.VMEM)
     result = pl.pallas_call(
         functools.partial(kernel, dims),
-        out_shape=jax.ShapeDtypeStruct((share, orient), f32),
-        in_specs=[vmem, pl.BlockSpec(memory_space=pl.ANY), vmem],
-        out_specs=vmem,
+        out_shape=pltpu.VMEM((share, orient), f32),
+        in_specs=[pl.BlockSpec(memory_space=pl.ANY)] * 3,
         scratch_shapes=[
+            pltpu.VMEM((fr * rows, lanes), jnp.int32),
+            pltpu.VMEM((rows, lanes), jnp.int32),
             pltpu.VMEM((orient * band, lanes), jnp.int32),
             pltpu.VMEM((orient, depth), bf16),
-            pltpu.VMEM((high + STRIDE_ROWS, fr, lanes), f32),
+            pltpu.VMEM((groups, high + STRIDE_ROWS, fr // groups, lanes), f32),
             pltpu.VMEM((2, PASSES, fr, lanes), bf16),
             pltpu.VMEM((2, PASSES, fr, lanes), bf16),
             pltpu.VMEM((nf * fr, depth), bf16),
@@ -437,6 +491,10 @@
             pltpu.VMEM((groups, sg, 128), f32),
             pltpu.VMEM((groups, no, sg, 128), f32),
             pltpu.VMEM((1, orient), f32),
+            pltpu.VMEM((high + STRIDE_ROWS, fr // groups, 2 * lanes), bf16),
+            pltpu.VMEM((high + STRIDE_ROWS, fr // groups, 2 * lanes), f32),
+            dma((2,)),
+            pltpu.SemaphoreType.REGULAR((max(nm, no),)),
             dma((orient // SLICE_CHUNK,)),
             dma((2, groups)),
             dma((2, groups)),

time: 74.4 us -> 70 us (0.941)
  Pallas kernels: 72.6 us -> 69.2 us
  local copies, waits for them, and re-layouts: 1.67 us -> 0.71 us
    pallas_call x1, Pallas kernels: 72.6 us -> 69.2 us  [body(): pl.pallas_call(functools.partial(kernel, dims), out_shape=pltpu.VMEM((sha...]
    unnamed x1, local copies, waits for them, and re-layouts: 1.67 us -> 0.71 us
where the time goes in v2:
time: 70 us; the launch traced here: 69.9 us
  Pallas kernels  69.2 us (99%)
  local copies, waits for them, and re-layouts  0.71 us (1%)
    pallas_call x1, Pallas kernels, body(): pl.pallas_call(functools.partial(kernel, dims), out_shape=pltpu.VMEM((sha...  69.2 us

profile of v2, /device:TPU:0, one launch (start us, length us, event | category | flops | bytes accessed | tf_op | source)
XLA Modules:
  0.0 69.9 jit_solution(8499133190897571213)
XLA Ops:
  0.0 69.2 %shard_map.37 = f32[64,1024]{1,0:T(8,128)S(1)} custom-call(s32[2048,128]{1,0:T(8,128)} %bitcast.5, s32[16384,128]{1,0:T(8,128)} %bitcast.4, s32[32,128]{1,0:T(8,128)} %mask_h.1), custom_call_target="tpu_custom_call" | custom-call | tf_op jit(solution)/shard_map/pallas_call | solution.py:470
  69.2 0.7 %copy.5 = f32[1,64,1024]{2,1,0:T(8,128)} copy(f32[1,64,1024]{2,1,0:T(8,128)S(1)} %bitcast.3) | data formatting | bytes 524288

commit v3 on v2

--- a/solution.py
+++ b/solution.py
@@ -34,7 +34,7 @@
 
 
 def group_count(nm, no, fr):
-    count = 4
+    count = 2
     while count > 1 and (nm > no or no % nm or fr % (16 * count)):
         count //= 2
     return count

time: 70 us -> 66.1 us (0.944)
  Pallas kernels: 69.2 us -> 65.2 us
    pallas_call x1, Pallas kernels: 69.2 us -> 65.2 us  [body(): pl.pallas_call(functools.partial(kernel, dims), out_shape=pltpu.VMEM((sha...]
where the time goes in v3:
time: 66.1 us; the launch traced here: 65.9 us
  Pallas kernels  65.2 us (99%)
  local copies, waits for them, and re-layouts  0.71 us (1%)
    pallas_call x1, Pallas kernels, body(): pl.pallas_call(functools.partial(kernel, dims), out_shape=pltpu.VMEM((sha...  65.2 us

profile of v3, /device:TPU:0, one launch (start us, length us, event | category | flops | bytes accessed | tf_op | source)
XLA Modules:
  0.0 65.9 jit_solution(5328011583217441580)
XLA Ops:
  0.0 65.2 %shard_map.37 = f32[64,1024]{1,0:T(8,128)S(1)} custom-call(s32[2048,128]{1,0:T(8,128)} %bitcast.5, s32[16384,128]{1,0:T(8,128)} %bitcast.4, s32[32,128]{1,0:T(8,128)} %mask_h.1), custom_call_target="tpu_custom_call" | custom-call | tf_op jit(solution)/shard_map/pallas_call | solution.py:470
  65.2 0.7 %copy.5 = f32[1,64,1024]{2,1,0:T(8,128)} copy(f32[1,64,1024]{2,1,0:T(8,128)S(1)} %bitcast.3) | data formatting | bytes 524288

commit v4 on v3

--- a/solution.py
+++ b/solution.py
@@ -434,18 +434,19 @@
     for c in range(chunks):
         task(-1.0 if c < early else 0.6 + (1.0 if 4 * c >= 3 * chunks else 0.0), slice_chunk, c)
     for g in range(groups):
+        tail = g == groups - 1
         task(g, diffuse, g)
         task(g + 0.1, first_hop, g)
-        task(g + 1.2, second_hop, g)
+        task(g + 0.7, second_hop, g)
         for k in range(1, hops):
-            task(g + 2.2 + 0.5 * (k - 1), later_hop, k, g)
-        task(g + 2.3 + 0.5 * (hops - 2), later_hop, hops, g)
+            task(g + (0.95 if tail else 1.15) + 0.01 * k, later_hop, k, g)
+        task(g + (1.1 if tail else 1.8), later_hop, hops, g)
         for t in range(tiles):
-            task(g + 2.4 + 0.5 * (hops - 2), multiply, g, t)
+            task(g + (1.15 if tail else 1.85), multiply, g, t)
         for t in range(tiles):
-            task(g + 3.3 + 0.5 * (hops - 2), reduce_frm, g, t)
-        task(g + 4.2 + 0.5 * (hops - 2), reduce_mod, g)
-        task(g + 4.9 + 0.5 * (hops - 2), finish, g)
+            task(g + (1.4 if tail else 2.05), reduce_frm, g, t)
+        task(g + (1.6 if tail else 2.3), reduce_mod, g)
+        task(g + (1.8 if tail else 2.5), finish, g)
     for _, _, call, args in sorted(tasks, key=lambda entry: entry[:2]):
         call(*args)
     for copy in pending:

time: 66.1 us -> 59.9 us (0.906)
  Pallas kernels: 65.2 us -> 59.1 us
    pallas_call x1, Pallas kernels: 65.2 us -> 59.1 us  [body(): pl.pallas_call(functools.partial(kernel, dims), out_shape=pltpu.VMEM((sha...]
where the time goes in v4:
time: 59.9 us; the launch traced here: 59.8 us
  Pallas kernels  59.1 us (99%)
  local copies, waits for them, and re-layouts  0.71 us (1%)
    pallas_call x1, Pallas kernels, body(): pl.pallas_call(functools.partial(kernel, dims), out_shape=pltpu.VMEM((sha...  59.1 us

profile of v4, /device:TPU:0, one launch (start us, length us, event | category | flops | bytes accessed | tf_op | source)
XLA Modules:
  0.0 59.8 jit_solution(3435176743387618596)
XLA Ops:
  0.0 59.1 %shard_map.37 = f32[64,1024]{1,0:T(8,128)S(1)} custom-call(s32[2048,128]{1,0:T(8,128)} %bitcast.5, s32[16384,128]{1,0:T(8,128)} %bitcast.4, s32[32,128]{1,0:T(8,128)} %mask_h.1), custom_call_target="tpu_custom_call" | custom-call | tf_op jit(solution)/shard_map/pallas_call | solution.py:471
  59.1 0.7 %copy.5 = f32[1,64,1024]{2,1,0:T(8,128)} copy(f32[1,64,1024]{2,1,0:T(8,128)S(1)} %bitcast.3) | data formatting | bytes 524288
